TPU v7x, 128 devices: a whole 4x4x4 slice. The times are simulated.
128 devices in a mesh: sect: 4 (over x), space: 32 (over z, y, core).
Axes of the slice: x: 4, y: 4, z: 4, core: 2. Of those that a mesh axis runs over, the one named last changes fastest.
Arguments:
- dist: bfloat16 [8000, 65536], P('sect', 'space'), may hold values from 0.25 to 4
- velocity: float32 [3, 8000], P(None, 'sect'), may hold values from -1.5 to 1.5
- quad_weight: float32 [8000], P('sect'), may hold values from 0.5 to 2
- collision_rate: float32 [65536], P('space'), may hold values from 0.1 to 0.9
- ghost_source: int32 [8192], P('space'), may hold values from 0 to 2047
- ghost_owner: int32 [8192, 1], P('space'), may hold values from 0 to 31; in each aligned block of 256 rows (0 to 255, 256 to 511, ...) at most 16 rows name the same one
- wall_cell: int32 [32, 32, 16], P('space'), may hold values from 0 to 2047
- plenum_moments: float32 [16384, 20], P('space'), may hold values from -6 to 6
- iface_cell: int32 [16384], P('space'), may hold values from 0 to 65535, as said below
Outputs:
- relaxed: bfloat16 [8000, 65536], P('sect', 'space')
Inputs may be any that keep to these rules, and one draw needn't show every extreme that they name: `ghost_owner`: in the rows of one slab no owner is named more than 16 times, a bound that some block reaches. `iface_cell`: distinct gap cells.
All inputs are finite; a program needn't handle non-finite values.
Results may differ from a plain program's by a relative error of at most 0.0065.
Values may be sent and summed in bfloat16 or wider, within the bound.
A program may use at most 192 MiB of HBM per device.

v0:
```python
import jax
import jax.numpy as jnp
from jax import lax
from jax.sharding import PartitionSpec as P

NV = 8000
MOMENTS = 20
COURANT_SCALE = 0.6
ES_SHIFT = -0.5
WALL_SHARE = 0.5
ORDER_TWO = ((0, 0), (1, 1), (2, 2), (0, 1), (0, 2), (1, 2))
ORDER_THREE = (
    (0, 0, 0),
    (1, 1, 1),
    (2, 2, 2),
    (0, 0, 1),
    (0, 0, 2),
    (1, 1, 0),
    (1, 1, 2),
    (2, 2, 0),
    (2, 2, 1),
    (0, 1, 2),
)
RECON_NORMS = (
    1.0,
    1.0,
    1.0,
    1.0,
    2.0,
    2.0,
    2.0,
    1.0,
    1.0,
    1.0,
    6.0,
    6.0,
    6.0,
    2.0,
    2.0,
    2.0,
    2.0,
    2.0,
    2.0,
    1.0,
)


def with_halo(shard, sides, width):
    for axis, dim in sides:
        count, length = (lax.axis_size(axis), shard.shape[dim])
        up = [(i, (i + 1) % count) for i in range(count - 1)]
        down = [(j, i) for i, j in up]
        last = lax.slice_in_dim(shard, length - width, length, axis=dim)
        first = lax.slice_in_dim(shard, 0, width, axis=dim)
        before = lax.ppermute(last, axis, up)
        after = lax.ppermute(first, axis, down)
        shard = jnp.concatenate([before, shard, after], axis=dim)
    return shard


def hermite(velocity):
    unity_row = jnp.ones_like(velocity[0])
    stacked = [unity_row, velocity[0], velocity[1], velocity[2]]
    for i, j in ORDER_TWO:
        element = velocity[i] * velocity[j]
        if i == j:
            element = element - 1.0
        stacked.append(element)
    for i, j, k in ORDER_THREE:
        element = velocity[i] * velocity[j] * velocity[k]
        if i == j:
            element = element - velocity[k]
        if i == k:
            element = element - velocity[j]
        if j == k:
            element = element - velocity[i]
        stacked.append(element)
    return jnp.stack(stacked)


def moment_basis(velocity, weight):
    return (hermite(velocity) * (weight / NV)[None, :]).astype(jnp.bfloat16)


def recon_basis(velocity):
    norms = jnp.array(RECON_NORMS, dtype=jnp.float32)
    return (hermite(velocity) / norms[:, None]).T.astype(jnp.bfloat16)


def transport(padded, courant):
    left = padded[:, :-2].astype(jnp.float32)
    centre = padded[:, 1:-1].astype(jnp.float32)
    right = padded[:, 2:].astype(jnp.float32)
    ahead = jnp.maximum(courant, 0.0)
    behind = jnp.minimum(courant, 0.0)
    return (centre - ahead * (centre - left) - behind * (right - centre)).astype(jnp.bfloat16)


def es_targets(moments):
    density = moments[0]
    moving = [moments[1], moments[2], moments[3]]
    trace_sum = moments[4] + moments[5] + moments[6]
    second = [[None, None, None], [None, None, None], [None, None, None]]
    for n, (i, j) in enumerate(ORDER_TWO):
        element = (1.0 - ES_SHIFT) * moments[4 + n]
        if i == j:
            element = element + ES_SHIFT * trace_sum / 3.0
        second[i][j] = element
        second[j][i] = element
    stacked = [density] + moving + [second[i][j] for i, j in ORDER_TWO]
    for n, (i, j, k) in enumerate(ORDER_THREE):
        stacked.append(
            0.5 * moments[10 + n]
            + (moving[i] * second[j][k] + moving[j] * second[i][k] + moving[k] * second[i][j])
            / density
        )
    return jnp.stack(stacked)


def slot_places(owner, peers, capacity):
    marks = (owner[:, None] == jnp.arange(peers, dtype=jnp.int32)[None, :]).astype(jnp.int32)
    before = jnp.cumsum(marks, axis=0) - marks
    slot = jnp.sum(marks * before, axis=1)
    return owner * capacity + slot


def add_block(carry, rows, cells, base, width):
    summed, hit = carry
    local = cells - base
    onehot = (local[:, None] == jnp.arange(width, dtype=jnp.int32)[None, :]).astype(jnp.float32)
    summed = summed + jnp.einsum("ka,kc->ac", rows, onehot, precision=lax.Precision.HIGHEST)
    hit = hit + jnp.sum(onehot, axis=0)
    return (summed, hit)


def fold_rows(carry, pieces, base, width):
    rows, cells = pieces
    count = rows.shape[0]
    blocks = (rows.reshape(count // 512, 512, rows.shape[1]), cells.reshape(count // 512, 512))

    def advance(inner, items):
        return (add_block(inner, items[0], items[1], base, width), None)

    carry, unused = lax.scan(advance, carry, blocks)
    return carry


def inject(closure, plenum_moments, iface_cell, base):
    width = closure.shape[1]
    start_state = (jnp.zeros((MOMENTS, width), jnp.float32), jnp.zeros((width,), jnp.float32))
    fluid, hit = fold_rows(
        start_state,
        (
            lax.all_gather(plenum_moments.astype(jnp.bfloat16), "space", axis=0, tiled=True).astype(
                jnp.float32
            ),
            lax.all_gather(iface_cell, "space", axis=0, tiled=True),
        ),
        base,
        width,
    )
    return closure + hit[None, :] * (fluid - closure)


def per_device(
    dist,
    velocity,
    quad_weight,
    collision_rate,
    ghost_source,
    ghost_owner,
    wall_cell,
    plenum_moments,
    iface_cell,
):
    cells = dist.shape[1]
    courant = (COURANT_SCALE * velocity[0])[:, None]
    padded = with_halo(dist, (("space", 1),), 1)
    read = transport(padded, courant)
    partial_moments = jnp.dot(
        moment_basis(velocity, quad_weight), read, preferred_element_type=jnp.float32
    )
    slab_base = lax.axis_index("space") * cells
    moments = lax.psum(partial_moments, "sect")
    targets = inject(es_targets(moments), plenum_moments, iface_cell, slab_base).astype(
        jnp.bfloat16
    )
    recon = recon_basis(velocity)
    equilibrium = jnp.dot(recon, targets, preferred_element_type=jnp.float32)
    peers = lax.axis_size("space")
    capacity = wall_cell.shape[2]
    slots = peers * capacity
    places = slot_places(ghost_owner[:, 0], peers, capacity)
    walls = wall_cell.reshape(slots)
    picked = jnp.take(equilibrium, ghost_source, axis=1)
    outgoing = jnp.zeros((picked.shape[0], slots), jnp.float32).at[:, places].set(picked)
    arrived = lax.all_to_all(outgoing, "space", split_axis=1, concat_axis=1, tiled=True)
    wall_sum = jnp.zeros((picked.shape[0], cells), jnp.float32).at[:, walls].add(arrived)
    rate = collision_rate[None, :]
    current = read.astype(jnp.float32)
    return (current + rate * (equilibrium - current) + WALL_SHARE * wall_sum).astype(jnp.bfloat16)


def solution(mesh):
    in_specs = (
        P("sect", "space"),
        P(None, "sect"),
        P("sect"),
        P("space"),
        P("space"),
        P("space", None),
        P("space", None, None),
        P("space", None),
        P("space"),
    )
    out_specs = P("sect", "space")
    return jax.shard_map(
        per_device, mesh=mesh, in_specs=in_specs, out_specs=out_specs, check_vma=False
    )
```

profile of v0, /device:TPU:0, one launch (start us, length us, event | category | flops | bytes accessed | tf_op | source)
XLA Modules:
  0.0 426.5 jit_solution(15446391911328866115)
XLA Ops:
  10.6 1.5 multiply_subtract_fusion.2
  12.1 1.5 multiply_maximum_fusion
  19.3 30.4 %all-gather = s32[32,1,512]{2,1,0:T(1,128)S(1)} all-gather(s32[1,1,512]{2,1,0:T(1,128)} %bitcast.62), channel_id=1, replica_groups=mesh['sect'=4,'space'=32] {'space'}, dimensions={0}, use_global_device_ids=true | all-gather | bytes 67584 | tf_op jit(solution)/shard_map/all_gather | solution.py:157
  49.7 22.7 %all_gather.6 = bf16[16384,20]{0,1:T(8,128)(2,1)S(1)} all-gather(bf16[512,20]{0,1:T(8,128)(2,1)S(1)} %convert_element_type.49), channel_id=1, replica_groups=mesh['sect'=4,'space'=32] {'space'}, dimensions={0}, use_global_device_ids=true | all-gather | bytes 675840 | tf_op jit(solution)/shard_map/all_gather | solution.py:154
  73.6 118.8 %while.13 = (s32[]{:T(128)}, f32[20,2048]{1,0:T(8,128)}, f32[2048]{0:T(1024)S(1)}, f32[32,512,20]{1,0,2:T(8,128)S(1)}, s32[32,512]{1,0:T(8,128)S(1)}, /*index=5*/s32[]{:T(128)}, s32[]{:T(128)}, s32[]{:T(128)}) while((s32[]{:T(128)}, f32[20,2048]{1,0:T(8,128)}, f32[2048]{0:T(1024)S(1)}, f32[32,512,20]{1,0,2:T(8,128)S(1)}, ...), condition=%wide.region_3.4_spmd.clone, body=%wide.region_1.3_spmd.clone.sunk | while | flops 255937024 | bytes 491636 | solution.py:144
  74.4 2.2 fusion.49
  77.2 3.1 fusion.49
  81.0 3.1 fusion.49
  84.7 3.1 fusion.49
  88.4 3.1 fusion.49
  92.2 3.1 fusion.49
  95.9 3.1 fusion.49
  99.6 3.1 fusion.49
  103.4 3.1 fusion.49
  107.1 3.1 fusion.49
  110.9 3.1 fusion.49
  114.6 3.1 fusion.49
  118.3 3.1 fusion.49
  122.1 3.1 fusion.49
  125.8 3.1 fusion.49
  129.5 3.1 fusion.49
  133.3 3.1 fusion.49
  137.0 3.1 fusion.49
  140.7 3.1 fusion.49
  144.5 3.1 fusion.49
  148.2 3.1 fusion.49
  151.9 3.1 fusion.49
  155.7 3.1 fusion.49
  159.4 3.1 fusion.49
  163.2 3.1 fusion.49
  166.9 3.1 fusion.49
  170.6 3.1 fusion.49
  174.4 3.1 fusion.49
  178.1 3.1 fusion.49
  181.8 3.1 fusion.49
  185.6 3.1 fusion.49
  189.3 3.1 fusion.49
  193.1 2.4 stack.6
  195.5 17.9 %fusion.17 = f32[20,2048]{1,0:T(8,128)} fusion(f32[20,2000]{1,0:T(8,128)S(1)} %stack.6, f32[2000]{0:T(1024)} %broadcast_multiply_fusion, bf16[2000,2048]{1,0:T(8,128)(2,1)} %param.12, bf16[2000,1]{1,0:T(8,128)(2,1)S(1)} %collective-permute-done.1, bf16[2000,1]{1,0:T(8,128)(2,1)S(1)} %collective-permute-done, f32[2000]{0:T(1024)S(1)} %bitcast.57, ...), kind=kOutput, calls=%fused_computation.37 | convolution fusion | flops 229456000 | bytes 8547840 | tf_op jit(solution)/shard_map/dot_general | solution.py:180
  213.6 40.6 %all-reduce.2.cloned.1.call-done = f32[20,2048]{1,0:T(8,128)} async-done(((f32[20,2048]{1,0:T(8,128)}), f32[20,2048]{1,0:T(8,128)}) %all-reduce.2.cloned.1.call-update) | async-done | bytes 163856 | tf_op jit(solution)/shard_map/psum | solution.py:184
  260.2 8.0 %fusion.18 = f32[2000,2048]{1,0:T(8,128)} fusion(f32[20,2048]{1,0:T(8,128)S(1)} %stack.7, f32[20,2048]{1,0:T(8,128)S(1)} %copy-done.1, f32[20,2000]{1,0:T(8,128)S(1)} %stack.6, f32[20]{0:T(128)S(1)} %copy-done.4, f32[2048]{0:T(1024)S(1)} %get-tuple-element.38), kind=kOutput, calls=%fused_computation.38 | convolution fusion | flops 164083840 | bytes 16879952 | tf_op jit(solution)/shard_map/dot_general | solution.py:189
  268.3 17.6 %copy.30 = f32[2000,2048]{0,1:T(8,128)} copy(f32[2000,2048]{1,0:T(8,128)} %fusion.18) | data formatting | bytes 32768000 | tf_op jit(solution)/shard_map/dot_general | solution.py:189
  285.9 8.0 %scatter_custom_fusion = f32[2000,512]{0,1:T(8,128)} fusion(s32[256]{0:T(256)} %bitcast.64, f32[]{:T(128)} %constant.25.clone.1, f32[]{:T(128)} %constant.73.clone.1, pred[256]{0:T(512)(128)(4,1)S(1)} %compare_and_fusion, f32[2000,2048]{0,1:T(8,128)} %copy.30, s32[1024]{0:T(1024)S(1)} %pad_clamp_fusion), kind=kCustom, calls=%fused_computation.28 | custom fusion | flops 512000 | bytes 20878592 | tf_op jit(solution)/shard_map/scatter | solution.py:196
  293.9 7.4 %all-to-all-start = ((f32[2000,32,16]{0,2,1:T(8,128)}), f32[2000,32,16]{0,2,1:T(8,128)}, u32[]{:S(2)}, u32[]{:S(2)}) async-start(f32[2000,32,16]{0,2,1:T(8,128)} %bitcast.49), calls=%async_computation | async-start | bytes 8388608 | tf_op jit(solution)/shard_map/all_to_all | solution.py:197
  301.4 53.8 %all-to-all-done = f32[2000,32,16]{0,2,1:T(8,128)} async-done(((f32[2000,32,16]{0,2,1:T(8,128)}), f32[2000,32,16]{0,2,1:T(8,128)}, u32[]{:S(2)}, u32[]{:S(2)}) %all-to-all-start) | async-done | bytes 4096032 | tf_op jit(solution)/shard_map/all_to_all | solution.py:197
  355.2 15.2 %scatter_custom_fusion.1 = f32[2000,2048]{0,1:T(8,128)} fusion(s32[512]{0:T(512)S(1)} %bitcast.63, f32[512,2000]{1,0:T(8,128)} %bitcast.11, f32[]{:T(128)} %constant.25.clone.1), kind=kCustom, calls=%fused_computation.24 | custom fusion | flops 1024000 | bytes 16384512 | tf_op jit(solution)/shard_map/scatter-add | solution.py:198
  370.4 17.6 %copy.31 = f32[2000,2048]{1,0:T(8,128)} copy(f32[2000,2048]{0,1:T(8,128)} %scatter_custom_fusion.1) | data formatting | bytes 32768000 | tf_op jit(solution)/shard_map/scatter-add | solution.py:198
  388.0 31.7 %fusion.5 = bf16[2000,2048]{1,0:T(8,128)(2,1)} fusion(f32[2000,2048]{1,0:T(8,128)} %fusion.18, f32[2000,2048]{1,0:T(8,128)} %copy.31, f32[2048]{0:T(1024)S(1)} %copy-done.2, bf16[2000,1]{1,0:T(8,128)(2,1)S(1)} %collective-permute-done.1, bf16[2000,2048]{1,0:T(8,128)(2,1)} %param.12, f32[2000]{0:T(1024)S(1)} %bitcast.58, ...), kind=kLoop, calls=%fused_computation.19 | loop fusion | flops 94208000 | bytes 49184192 | tf_op jit(solution)/shard_map/convert_element_type | solution.py:201
  (175 shorter events, 37.5 us)
Async XLA Ops:
  6.5 186.6 %copy-start = (f32[3,2000]{1,0:T(4,128)S(1)}, f32[3,2000]{1,0:T(4,128)}, u32[]{:S(2)}) copy-start(f32[3,2000]{1,0:T(4,128)} %param.13) | copy-start | bytes 72004
  6.5 247.7 %all-reduce.2.cloned.1.call-start = ((), (), s32[]{:S(2)}) async-start(), calls=%async_computation.1 | async-start | bytes 393216 | tf_op jit(solution)/shard_map/psum | solution.py:184
  8.0 187.5 %collective-permute-start = (bf16[2000,1]{1,0:T(8,128)(2,1)S(1)}, bf16[2000,1]{1,0:T(8,128)(2,1)S(1)}, u32[]{:S(2)}, u32[]{:S(2)}) collective-permute-start(bf16[2000,1]{1,0:T(8,128)(2,1)S(1)} %get-tuple-element.100), channel_id=1, source_target_pairs={{0,1},{1,2},{2,3},{3,4},{4,5},{5,6},{6,7},{7,8},{8,9},{9,10},{10,1... | collective-permute-start | bytes 12008 | tf_op jit(solution)/shard_map/ppermute | solution.py:55
  9.3 186.2 %collective-permute-start.1 = (bf16[2000,1]{1,0:T(8,128)(2,1)S(1)}, bf16[2000,1]{1,0:T(8,128)(2,1)S(1)}, u32[]{:S(2)}, u32[]{:S(2)}) collective-permute-start(bf16[2000,1]{1,0:T(8,128)(2,1)S(1)} %get-tuple-element.101), channel_id=1, source_target_pairs={{1,0},{2,1},{3,2},{4,3},{5,4},{6,5},{7,6},{8,7},{9,8},{10,9},{11,1... | collective-permute-start | bytes 12008 | tf_op jit(solution)/shard_map/ppermute | solution.py:56
  195.5 18.0 %copy-start.5 = (s32[256]{0:T(256)S(1)}, s32[256]{0:T(256)}, u32[]{:S(2)}) copy-start(s32[256]{0:T(256)} %param.16) | copy-start | bytes 3076
  195.5 64.7 %copy-start.1 = (f32[20,2048]{1,0:T(8,128)S(1)}, f32[20,2048]{1,0:T(8,128)}, u32[]{:S(2)}) copy-start(f32[20,2048]{1,0:T(8,128)} %get-tuple-element.39) | copy-start | bytes 491524
  195.5 64.7 %copy-start.4 = (f32[20]{0:T(128)S(1)}, f32[20]{0:T(128)}, u32[]{:S(2)}) copy-start(f32[20]{0:T(128)} %constant.76) | copy-start | bytes 244
  285.9 15.4 %copy-start.3 = (s32[1,32,16]{1,2,0:T(8,128)S(1)}, s32[1,32,16]{1,2,0:T(8,128)}, u32[]{:S(2)}) copy-start(s32[1,32,16]{1,2,0:T(8,128)} %param.18) | copy-start | bytes 6148
  293.9 61.4 %all-to-all-start = ((f32[2000,32,16]{0,2,1:T(8,128)}), f32[2000,32,16]{0,2,1:T(8,128)}, u32[]{:S(2)}, u32[]{:S(2)}) async-start(f32[2000,32,16]{0,2,1:T(8,128)} %bitcast.49), calls=%async_computation | async-start | bytes 8388608 | tf_op jit(solution)/shard_map/all_to_all | solution.py:197
  370.4 17.6 %copy-start.2 = (f32[2048]{0:T(1024)S(1)}, f32[2048]{0:T(1024)}, u32[]{:S(2)}) copy-start(f32[2048]{0:T(1024)} %param.15) | copy-start | bytes 24580
Sparse Core Ops, SparseCore 0:
  213.6 40.5 all-reduce.1
where the time goes:
time: 429 us; the launch traced here: 426 us
  matrix products  124 us (29%)
  waiting for transfers between devices  94.4 us (22%)
  other arithmetic  87.5 us (20%)
  blocking collectives  53.1 us (12%)
  local copies, waits for them, and re-layouts  42.8 us (10%)
  between operations  13.6 us (3%)
  starting transfers between devices  10 us (2%)
    dot_general x32, matrix products, add_block(): jnp.einsum('ka,kc->ac', rows, onehot, precision=lax.Precision.HIGHEST)  98 us
    all_to_all x1, waiting for transfers between devices, per_device(): lax.all_to_all(outgoing, 'space', split_axis=1, concat_axis=1, tiled=True)  53.8 us
    psum x1, waiting for transfers between devices, per_device(): moments = lax.psum(partial_moments, 'sect')  40.6 us
    convert_element_type x1, other arithmetic, per_device(): (current + rate * (equilibrium - current) + WALL_SHARE * wall_sum).astype...  31.7 us
    all_gather x1, blocking collectives, inject(): lax.all_gather(iface_cell, 'space', axis=0, tiled=True)  30.4 us
    all_gather x1, blocking collectives, inject(): lax.all_gather(plenum_moments.astype(jnp.bfloat16), 'space', axis=0, tile...  22.7 us
    reduce_sum x32, other arithmetic, add_block(): hit = hit + jnp.sum(onehot, axis=0)  18.1 us
    dot_general x1, matrix products, per_device(): jnp.dot(moment_basis(velocity, quad_weight), read, preferred_element_type...  17.9 us
  transfers between devices with their start and end apart: 4, of which 2 were waited for; matrix products, arithmetic and copies ran while one was open for 31% of the time, Pallas kernels for 0%

commit v1 on v0

--- a/solution.py
+++ b/solution.py
@@ -181,7 +181,9 @@
         moment_basis(velocity, quad_weight), read, preferred_element_type=jnp.float32
     )
     slab_base = lax.axis_index("space") * cells
-    moments = lax.psum(partial_moments, "sect")
+    moments = partial_moments
+    for hop in (1, 2):
+        moments = moments + lax.ppermute(moments, "sect", [(dev, dev ^ hop) for dev in range(4)])
     targets = inject(es_targets(moments), plenum_moments, iface_cell, slab_base).astype(
         jnp.bfloat16
     )

time: 429 us -> 381 us (0.89)
  waiting for transfers between devices: 94.4 us -> 64 us
  between operations: 13.6 us -> 0.21 us
  other arithmetic: 87.5 us -> 81.4 us
    psum x1 -> x0, waiting for transfers between devices: 40.6 us -> none  [per_device(): moments = lax.psum(partial_moments, 'sect')]
    ppermute x0 -> x2, waiting for transfers between devices: none -> 10.4 us  [per_device(): lax.ppermute(moments, 'sect', [(dev, dev ^ hop) for dev in range(4)])]
    ppermute x0 -> x2, starting transfers between devices: none -> 4.85 us  [per_device(): lax.ppermute(moments, 'sect', [(dev, dev ^ hop) for dev in range(4)])]
    add x4, other arithmetic: 4.93 us -> 0.34 us  [es_targets(): 0.5 * moments[10 + n]]
  transfers between devices with their start and end apart: 4 -> 5, of which waited for: 2 -> 3; matrix products, arithmetic and copies ran while one was open for 31% -> 34% of each run, Pallas kernels for 0% -> 0%
where the time goes in v1:
time: 381 us; the launch traced here: 378 us
  matrix products  124 us (33%)
  other arithmetic  81.4 us (21%)
  waiting for transfers between devices  64 us (17%)
  blocking collectives  53.1 us (14%)
  local copies, waits for them, and re-layouts  42.6 us (11%)
  starting transfers between devices  12.7 us (3%)
    dot_general x32, matrix products, add_block(): jnp.einsum('ka,kc->ac', rows, onehot, precision=lax.Precision.HIGHEST)  98.2 us
    all_to_all x1, waiting for transfers between devices, per_device(): lax.all_to_all(outgoing, 'space', split_axis=1, concat_axis=1, tiled=True)  53.6 us
    convert_element_type x1, other arithmetic, per_device(): (current + rate * (equilibrium - current) + WALL_SHARE * wall_sum).astype...  31.7 us
    all_gather x1, blocking collectives, inject(): lax.all_gather(iface_cell, 'space', axis=0, tiled=True)  30.4 us
    all_gather x1, blocking collectives, inject(): lax.all_gather(plenum_moments.astype(jnp.bfloat16), 'space', axis=0, tile...  22.7 us
    reduce_sum x32, other arithmetic, add_block(): hit = hit + jnp.sum(onehot, axis=0)  18.1 us
    dot_general x1, local copies, waits for them, and re-layouts, per_device(): equilibrium = jnp.dot(recon, targets, preferred_element_type=jnp.float32)  17.6 us
    scatter-add x1, local copies, waits for them, and re-layouts, per_device(): jnp.zeros((picked.shape[0], cells), jnp.float32).at[:, walls].add(arrived)  17.6 us
  transfers between devices with their start and end apart: 5, of which 3 were waited for; matrix products, arithmetic and copies ran while one was open for 34% of the time, Pallas kernels for 0%

profile of v1, /device:TPU:0, one launch (start us, length us, event | category | flops | bytes accessed | tf_op | source)
XLA Modules:
  0.0 378.4 jit_solution(9924402573863985778)
XLA Ops:
  11.3 30.4 %all-gather = s32[32,1,512]{2,1,0:T(1,128)S(1)} all-gather(s32[1,1,512]{2,1,0:T(1,128)} %bitcast.62), channel_id=1, replica_groups=mesh['sect'=4,'space'=32] {'space'}, dimensions={0}, use_global_device_ids=true | all-gather | bytes 67584 | tf_op jit(solution)/shard_map/all_gather | solution.py:157
  41.6 22.7 %all_gather.6 = bf16[16384,20]{0,1:T(8,128)(2,1)S(1)} all-gather(bf16[512,20]{0,1:T(8,128)(2,1)S(1)} %convert_element_type.49), channel_id=1, replica_groups=mesh['sect'=4,'space'=32] {'space'}, dimensions={0}, use_global_device_ids=true | all-gather | bytes 675840 | tf_op jit(solution)/shard_map/all_gather | solution.py:154
  65.5 118.9 %while.13 = (s32[]{:T(128)}, f32[20,2048]{1,0:T(8,128)}, f32[2048]{0:T(1024)S(1)}, f32[32,512,20]{1,0,2:T(8,128)S(1)}, s32[32,512]{1,0:T(8,128)S(1)}, /*index=5*/s32[]{:T(128)}, s32[]{:T(128)}, s32[]{:T(128)}) while((s32[]{:T(128)}, f32[20,2048]{1,0:T(8,128)}, f32[2048]{0:T(1024)S(1)}, f32[32,512,20]{1,0,2:T(8,128)S(1)}, ...), condition=%wide.region_2.3_spmd.clone, body=%wide.region_0.2_spmd.clone.sunk | while | flops 255937024 | bytes 491636 | solution.py:144
  66.2 2.2 fusion.49
  69.0 3.1 fusion.49
  72.8 3.1 fusion.49
  76.5 3.1 fusion.49
  80.2 3.1 fusion.49
  84.0 3.1 fusion.49
  87.7 3.1 fusion.49
  91.5 3.1 fusion.49
  95.2 3.1 fusion.49
  99.0 3.1 fusion.49
  102.7 3.1 fusion.49
  106.5 3.1 fusion.49
  110.2 3.1 fusion.49
  113.9 3.1 fusion.49
  117.7 3.1 fusion.49
  121.4 3.1 fusion.49
  125.2 3.1 fusion.49
  128.9 3.1 fusion.49
  132.7 3.1 fusion.49
  136.4 3.1 fusion.49
  140.1 3.1 fusion.49
  143.9 3.1 fusion.49
  147.6 3.1 fusion.49
  151.4 3.1 fusion.49
  155.1 3.1 fusion.49
  158.9 3.1 fusion.49
  162.6 3.1 fusion.49
  166.3 3.1 fusion.49
  170.1 3.1 fusion.49
  173.8 3.1 fusion.49
  177.6 3.1 fusion.49
  181.3 3.1 fusion.49
  185.9 2.5 stack.6
  188.4 17.3 %fusion.17 = f32[20,2048]{1,0:T(8,128)S(1)} fusion(f32[20,2000]{1,0:T(8,128)S(1)} %stack.6, f32[2000]{0:T(1024)} %broadcast_multiply_fusion, bf16[2000,2048]{1,0:T(8,128)(2,1)} %param.12, bf16[2000,1]{1,0:T(8,128)(2,1)S(1)} %collective-permute-done.1, bf16[2000,1]{1,0:T(8,128)(2,1)S(1)} %collective-permute-done, f32[2000]{0:T(1024)S(1)} %bitcast.57, ...), kind=kOutput, calls=%fused_computation.37 | convolution fusion | flops 229456000 | bytes 8547840 | tf_op jit(solution)/shard_map/dot_general | solution.py:180
  207.3 5.7 %collective-permute-done.2 = f32[20,2048]{1,0:T(8,128)S(1)} collective-permute-done((f32[20,2048]{1,0:T(8,128)S(1)}, f32[20,2048]{1,0:T(8,128)S(1)}, u32[]{:S(2)}, u32[]{:S(2)}) %collective-permute-start.2) | collective-permute-done | bytes 163872 | tf_op jit(solution)/shard_map/ppermute | solution.py:186
  212.9 3.3 collective-permute-start.3
  216.2 4.8 %collective-permute-done.3 = f32[20,2048]{1,0:T(8,128)S(1)} collective-permute-done((f32[20,2048]{1,0:T(8,128)S(1)}, f32[20,2048]{1,0:T(8,128)S(1)}, u32[]{:S(2)}, u32[]{:S(2)}) %collective-permute-start.3) | collective-permute-done | bytes 163872 | tf_op jit(solution)/shard_map/ppermute | solution.py:186
  221.7 8.0 %fusion.18 = f32[2000,2048]{1,0:T(8,128)} fusion(f32[20,2048]{1,0:T(8,128)S(1)} %stack.7, f32[20,2048]{1,0:T(8,128)S(1)} %copy-done.1, f32[20,2000]{1,0:T(8,128)S(1)} %stack.6, f32[20]{0:T(128)S(1)} %copy-done.4, f32[2048]{0:T(1024)S(1)} %get-tuple-element.38), kind=kOutput, calls=%fused_computation.38 | convolution fusion | flops 164083840 | bytes 16879952 | tf_op jit(solution)/shard_map/dot_general | solution.py:191
  229.7 17.6 %copy.30 = f32[2000,2048]{0,1:T(8,128)} copy(f32[2000,2048]{1,0:T(8,128)} %fusion.18) | data formatting | bytes 32768000 | tf_op jit(solution)/shard_map/dot_general | solution.py:191
  247.4 7.6 %scatter_custom_fusion = f32[2000,512]{0,1:T(8,128)} fusion(s32[256]{0:T(256)S(1)} %bitcast.64, f32[]{:T(128)} %constant.25.clone.1, f32[]{:T(128)} %constant.73.clone.1, pred[256]{0:T(512)(128)(4,1)S(1)} %compare_and_fusion, f32[2000,2048]{0,1:T(8,128)} %copy.30, s32[1024]{0:T(1024)S(1)} %pad_clamp_fusion), kind=kCustom, calls=%fused_computation.28 | custom fusion | flops 512000 | bytes 20484616 | tf_op jit(solution)/shard_map/scatter | solution.py:198
  255.0 5.3 %all-to-all-start = ((f32[2000,32,16]{0,2,1:T(8,128)}), f32[2000,32,16]{0,2,1:T(8,128)}, u32[]{:S(2)}, u32[]{:S(2)}) async-start(f32[2000,32,16]{0,2,1:T(8,128)} %bitcast.49), calls=%async_computation | async-start | bytes 8388608 | tf_op jit(solution)/shard_map/all_to_all | solution.py:199
  260.4 53.6 %all-to-all-done = f32[2000,32,16]{0,2,1:T(8,128)} async-done(((f32[2000,32,16]{0,2,1:T(8,128)}), f32[2000,32,16]{0,2,1:T(8,128)}, u32[]{:S(2)}, u32[]{:S(2)}) %all-to-all-start) | async-done | bytes 4096032 | tf_op jit(solution)/shard_map/all_to_all | solution.py:199
  314.0 15.2 %scatter_custom_fusion.1 = f32[2000,2048]{0,1:T(8,128)} fusion(s32[512]{0:T(512)S(1)} %bitcast.63, f32[512,2000]{1,0:T(8,128)} %bitcast.11, f32[]{:T(128)} %constant.25.clone.1), kind=kCustom, calls=%fused_computation.24 | custom fusion | flops 1024000 | bytes 16384512 | tf_op jit(solution)/shard_map/scatter-add | solution.py:200
  329.2 17.6 %copy.31 = f32[2000,2048]{1,0:T(8,128)} copy(f32[2000,2048]{0,1:T(8,128)} %scatter_custom_fusion.1) | data formatting | bytes 32768000 | tf_op jit(solution)/shard_map/scatter-add | solution.py:200
  346.8 31.7 %fusion.5 = bf16[2000,2048]{1,0:T(8,128)(2,1)} fusion(f32[2000,2048]{1,0:T(8,128)} %fusion.18, f32[2000,2048]{1,0:T(8,128)} %copy.31, f32[2048]{0:T(1024)S(1)} %copy-done.2, bf16[2000,1]{1,0:T(8,128)(2,1)S(1)} %collective-permute-done.1, bf16[2000,2048]{1,0:T(8,128)(2,1)} %param.12, f32[2000]{0:T(1024)S(1)} %bitcast.58, ...), kind=kLoop, calls=%fused_computation.19 | loop fusion | flops 94208000 | bytes 49184192 | tf_op jit(solution)/shard_map/convert_element_type | solution.py:203
  (178 shorter events, 36.1 us)
Async XLA Ops:
  0.0 185.9 %copy-start = (f32[3,2000]{1,0:T(4,128)S(1)}, f32[3,2000]{1,0:T(4,128)}, u32[]{:S(2)}) copy-start(f32[3,2000]{1,0:T(4,128)} %param.13) | copy-start | bytes 72004
  1.4 186.9 %collective-permute-start = (bf16[2000,1]{1,0:T(8,128)(2,1)S(1)}, bf16[2000,1]{1,0:T(8,128)(2,1)S(1)}, u32[]{:S(2)}, u32[]{:S(2)}) collective-permute-start(bf16[2000,1]{1,0:T(8,128)(2,1)S(1)} %get-tuple-element.100), channel_id=1, source_target_pairs={{0,1},{1,2},{2,3},{3,4},{4,5},{5,6},{6,7},{7,8},{8,9},{9,10},{10,1... | collective-permute-start | bytes 12008 | tf_op jit(solution)/shard_map/ppermute | solution.py:55
  2.8 185.6 %collective-permute-start.1 = (bf16[2000,1]{1,0:T(8,128)(2,1)S(1)}, bf16[2000,1]{1,0:T(8,128)(2,1)S(1)}, u32[]{:S(2)}, u32[]{:S(2)}) collective-permute-start(bf16[2000,1]{1,0:T(8,128)(2,1)S(1)} %get-tuple-element.101), channel_id=1, source_target_pairs={{1,0},{2,1},{3,2},{4,3},{5,4},{6,5},{7,6},{8,7},{9,8},{10,9},{11,1... | collective-permute-start | bytes 12008 | tf_op jit(solution)/shard_map/ppermute | solution.py:56
  188.4 18.9 %copy-start.5 = (s32[256]{0:T(256)S(1)}, s32[256]{0:T(256)}, u32[]{:S(2)}) copy-start(s32[256]{0:T(256)} %param.16) | copy-start | bytes 3076
  188.4 33.3 %copy-start.1 = (f32[20,2048]{1,0:T(8,128)S(1)}, f32[20,2048]{1,0:T(8,128)}, u32[]{:S(2)}) copy-start(f32[20,2048]{1,0:T(8,128)} %get-tuple-element.39) | copy-start | bytes 491524
  188.4 33.3 %copy-start.4 = (f32[20]{0:T(128)S(1)}, f32[20]{0:T(128)}, u32[]{:S(2)}) copy-start(f32[20]{0:T(128)} %constant.76) | copy-start | bytes 244
  205.7 7.2 %collective-permute-start.2 = (f32[20,2048]{1,0:T(8,128)S(1)}, f32[20,2048]{1,0:T(8,128)S(1)}, u32[]{:S(2)}, u32[]{:S(2)}) collective-permute-start(f32[20,2048]{1,0:T(8,128)S(1)} %fusion.17), channel_id=1, source_target_pairs={{0,32},{32,0},{64,96},{96,64},{1,33},{33,1},{65,97},{97,65},{2,34}... | collective-permute-start | bytes 491528 | tf_op jit(solution)/shard_map/ppermute | solution.py:186
  212.9 8.1 %collective-permute-start.3 = (f32[20,2048]{1,0:T(8,128)S(1)}, f32[20,2048]{1,0:T(8,128)S(1)}, u32[]{:S(2)}, u32[]{:S(2)}) collective-permute-start(f32[20,2048]{1,0:T(8,128)S(1)} %add.235), channel_id=1, source_target_pairs={{0,64},{32,96},{64,0},{96,32},{1,65},{33,97},{65,1},{97,33},{2,66}... | collective-permute-start | bytes 491528 | tf_op jit(solution)/shard_map/ppermute | solution.py:186
  247.4 12.9 %copy-start.3 = (s32[1,32,16]{1,2,0:T(8,128)S(1)}, s32[1,32,16]{1,2,0:T(8,128)}, u32[]{:S(2)}) copy-start(s32[1,32,16]{1,2,0:T(8,128)} %param.18) | copy-start | bytes 6148
  255.0 59.0 %all-to-all-start = ((f32[2000,32,16]{0,2,1:T(8,128)}), f32[2000,32,16]{0,2,1:T(8,128)}, u32[]{:S(2)}, u32[]{:S(2)}) async-start(f32[2000,32,16]{0,2,1:T(8,128)} %bitcast.49), calls=%async_computation | async-start | bytes 8388608 | tf_op jit(solution)/shard_map/all_to_all | solution.py:199
  329.2 17.6 %copy-start.2 = (f32[2048]{0:T(1024)S(1)}, f32[2048]{0:T(1024)}, u32[]{:S(2)}) copy-start(f32[2048]{0:T(1024)} %param.15) | copy-start | bytes 24580
